TPU v7x, 32 devices: a whole 2x2x4 slice. The times are simulated.
32 devices in a mesh: groups: 2 (over x), ep: 16 (over z, y, core).
Axes of the slice: x: 2, y: 2, z: 4, core: 2. Of those that a mesh axis runs over, the one named last changes fastest.
Arguments:
- tokens: bfloat16 [512, 3072], P(('groups', 'ep')), parts along dimension 0, may hold values from -6 to 6
- routes: int32 [512, 2], P(('groups', 'ep')), parts along dimension 0, may hold values from 0 to 3, all different within a row
- route_weights: float32 [512, 2], P(('groups', 'ep')), parts along dimension 0, may hold values from 0.1 to 1
- live_counts: int32 [32], P(('groups', 'ep')), parts along dimension 0, may hold values from 8 to 16, as said below
- w_gate: bfloat16 [3072, 32768], P(None, 'ep'), may hold values from -0.109375 to 0.109375
- w_up: bfloat16 [3072, 32768], P(None, 'ep'), may hold values from -0.109375 to 0.109375
- w_down: bfloat16 [32768, 3072], P('ep'), may hold values from -0.0625 to 0.0625
Outputs:
- mixed: bfloat16 [512, 3072], P(('groups', 'ep')), parts along dimension 0
There are 2 independent parts, one for each index of `groups`. A program takes and returns all parts, laid end to end along the dimension named above; an argument that names none is the same for every part. Nothing has to cross between parts.
Inputs may be any that keep to these rules, and one draw needn't show every extreme that they name: `routes`: each token names two different experts. The live tokens of a device are its first live_counts rows; some device has all 16 live and some has 8.
All inputs are finite; a program needn't handle non-finite values.
Results may differ from a plain program's by a relative error of at most 0.0057.
Values may be sent and summed in bfloat16 or wider, within the bound.
A program may use at most 128 MiB of HBM per device.

v0:
```python
import jax
import jax.numpy as jnp
from jax import lax
from jax.sharding import PartitionSpec as P

EXPERTS = 4


def expert_rows(row_block, w_gate, w_up, w_down):
    gate = jnp.dot(row_block, w_gate, preferred_element_type=jnp.float32)
    upward = jnp.dot(row_block, w_up, preferred_element_type=jnp.float32)
    hidden = (jax.nn.silu(gate) * upward).astype(jnp.bfloat16)
    return jnp.dot(hidden, w_down, preferred_element_type=jnp.float32).astype(jnp.bfloat16)


def local(tokens, routes, route_weights, live_counts, w_gate, w_up, w_down):
    devices = lax.axis_size("ep")
    partners = devices // EXPERTS
    tok_rows, features = tokens.shape
    all_rows = devices * tok_rows
    is_live = jnp.arange(tok_rows, dtype=jnp.int32) < live_counts[0]
    chosen = (routes[:, :, None] == jnp.arange(EXPERTS, dtype=jnp.int32)[None, None, :]) & is_live[
        :, None, None
    ]
    assigned = chosen.reshape(tok_rows * 2, EXPERTS).astype(jnp.int32)
    earlier = jnp.cumsum(assigned, axis=0) - assigned
    slot_index = jnp.sum(earlier * assigned, axis=1).reshape(tok_rows, 2)
    target = jnp.where(is_live[:, None], routes * tok_rows + slot_index, -1)
    select = jnp.any(
        jnp.arange(EXPERTS * tok_rows, dtype=jnp.int32)[:, None, None] == target[None, :, :], axis=2
    )
    outbox = jnp.dot(
        select.astype(jnp.bfloat16), tokens, preferred_element_type=jnp.float32
    ).astype(jnp.bfloat16)
    outbox = outbox.reshape(EXPERTS, tok_rows, features)
    outgoing = jnp.broadcast_to(outbox[:, None], (EXPERTS, partners, tok_rows, features)).reshape(
        devices, tok_rows, features
    )
    received = lax.all_to_all(outgoing, "ep", split_axis=0, concat_axis=0, tiled=True)
    flat_rows = received.reshape(all_rows, features)
    partial_value = expert_rows(flat_rows, w_gate, w_up, w_down)
    returned = lax.all_to_all(
        partial_value.reshape(devices, tok_rows, features),
        "ep",
        split_axis=0,
        concat_axis=0,
        tiled=True,
    )
    summed = jnp.sum(
        returned.reshape(EXPERTS, partners, tok_rows, features).astype(jnp.float32), axis=1
    )
    gathered = summed.reshape(EXPERTS * tok_rows, features)
    picked = gathered[jnp.maximum(target, 0)]
    mixed = (
        route_weights[:, 0][:, None] * picked[:, 0] + route_weights[:, 1][:, None] * picked[:, 1]
    )
    mixed = jnp.where(is_live[:, None], mixed, jnp.float32(0.0))
    return mixed.astype(jnp.bfloat16)


def solution(mesh):
    in_specs = (
        P(("groups", "ep"), None),
        P(("groups", "ep"), None),
        P(("groups", "ep"), None),
        P(("groups", "ep")),
        P(None, "ep"),
        P(None, "ep"),
        P("ep", None),
    )
    out_specs = P(("groups", "ep"), None)
    return jax.shard_map(local, mesh=mesh, in_specs=in_specs, out_specs=out_specs, check_vma=False)
```

profile of v0, /device:TPU:15, one launch (start us, length us, event | category | flops | bytes accessed | tf_op | source)
XLA Modules:
  0.0 114.2 jit_solution(10619593889007973785)
XLA Ops:
  0.0 0.0 copy-start
  0.7 0.1 broadcast_in_dim.42.clone
  0.8 0.1 and.11
  0.9 0.8 copy.24
  1.6 0.1 eq.30
  1.7 0.1 fusion.8
  1.8 0.1 reduce_window_sum.11
  1.9 0.2 select_reduce_fusion
  2.0 0.1 reshape.33
  2.1 0.1 copy.26
  2.2 0.7 broadcast_maximum_fusion
  2.9 0.1 fusion.6
  3.0 0.0 copy-done
  3.0 0.3 convolution_convert_fusion.1
  3.3 0.2 broadcast_in_dim.45
  3.5 42.4 %all_to_all.10 = bf16[16,16,3072]{2,1,0:T(8,128)(2,1)S(1)} all-to-all(bf16[16,16,3072]{2,1,0:T(8,128)(2,1)S(1)} %bitcast.38), channel_id=1, replica_groups=mesh['groups'=2,'ep'=16] {'ep'}, dimensions={0} | all-to-all | bytes 3145728 | tf_op jit(solution)/shard_map/all_to_all | solution.py:39
  45.9 7.8 %fusion.11 = f32[256,2048]{1,0:T(8,128)} fusion(bf16[256,3072]{1,0:T(8,128)(2,1)S(1)} %bitcast.39, bf16[3072,2048]{1,0:T(8,128)(2,1)} %param.11), kind=kOutput, calls=%fused_computation.27 | convolution fusion | flops 3221225472 | bytes 16252928 | tf_op jit(solution)/shard_map/dot_general | solution.py:10
  53.7 16.9 %convolution_convert_fusion = bf16[256,3072]{1,0:T(8,128)(2,1)} fusion(bf16[2048,3072]{1,0:T(8,128)(2,1)} %param.13, bf16[256,3072]{1,0:T(8,128)(2,1)S(1)} %bitcast.40, bf16[3072,2048]{1,0:T(8,128)(2,1)} %param.12, f32[256,2048]{1,0:T(8,128)} %fusion.11), kind=kOutput, calls=%fused_computation.1 | convolution fusion | flops 6446383104 | bytes 30408704 | tf_op jit(solution)/shard_map/dot_general | solution.py:13
  70.6 0.0 copy-start.1
  70.6 5.2 %all-to-all-start.1 = ((bf16[16,16,3072]{2,1,0:T(8,128)(2,1)}), bf16[16,16,3072]{2,1,0:T(8,128)(2,1)S(1)}, u32[]{:S(2)}, u32[]{:S(2)}) async-start(bf16[16,16,3072]{2,1,0:T(8,128)(2,1)} %bitcast.5), calls=%async_computation.1 | async-start | bytes 3145728 | tf_op jit(solution)/shard_map/all_to_all | solution.py:42
  75.7 0.1 copy.27
  75.8 0.1 reshape.41
  75.9 0.0 copy-done.1
  76.0 36.0 %all-to-all-done.1 = bf16[16,16,3072]{2,1,0:T(8,128)(2,1)S(1)} async-done(((bf16[16,16,3072]{2,1,0:T(8,128)(2,1)}), bf16[16,16,3072]{2,1,0:T(8,128)(2,1)S(1)}, u32[]{:S(2)}, u32[]{:S(2)}) %all-to-all-start.1) | async-done | bytes 1572896 | tf_op jit(solution)/shard_map/all_to_all | solution.py:42
  111.9 0.2 convert_reduce_fusion
  112.2 0.7 gather_fusion
  112.9 0.2 reshape.40
  113.1 0.3 fusion.10
  113.4 0.8 fusion.4
  (3 shorter events, 0.0 us)
Async XLA Ops:
  0.0 3.0 %copy-start = (bf16[16,3072]{1,0:T(8,128)(2,1)S(1)}, bf16[16,3072]{1,0:T(8,128)(2,1)}, u32[]{:S(2)}) copy-start(bf16[16,3072]{1,0:T(8,128)(2,1)} %param.7) | copy-start | bytes 294916
  70.6 5.4 %copy-start.1 = (f32[16,2]{0,1:T(2,128)S(1)}, f32[16,2]{0,1:T(2,128)}, u32[]{:S(2)}) copy-start(f32[16,2]{0,1:T(2,128)} %param.9) | copy-start | bytes 388
  70.6 41.4 %all-to-all-start.1 = ((bf16[16,16,3072]{2,1,0:T(8,128)(2,1)}), bf16[16,16,3072]{2,1,0:T(8,128)(2,1)S(1)}, u32[]{:S(2)}, u32[]{:S(2)}) async-start(bf16[16,16,3072]{2,1,0:T(8,128)(2,1)} %bitcast.5), calls=%async_computation.1 | async-start | bytes 3145728 | tf_op jit(solution)/shard_map/all_to_all | solution.py:42
where the time goes:
time: 114 us
  blocking collectives  42.4 us (37%)
  waiting for transfers between devices  36 us (32%)
  matrix products  25 us (22%)
  starting transfers between devices  5.18 us (5%)
  local copies, waits for them, and re-layouts  2.77 us (2%)
  other arithmetic  2.13 us (2%)
    all_to_all x1, blocking collectives, local(): lax.all_to_all(outgoing, 'ep', split_axis=0, concat_axis=0, tiled=True)  42.4 us
    all_to_all x1, waiting for transfers between devices, local(): lax.all_to_all(partial_value.reshape(devices, tok_rows, features), 'ep',...  36 us
    dot_general x1, matrix products, expert_rows(): jnp.dot(hidden, w_down, preferred_element_type=jnp.float32)  16.9 us
    dot_general x1, matrix products, expert_rows(): gate = jnp.dot(row_block, w_gate, preferred_element_type=jnp.float32)  7.78 us
    all_to_all x1, starting transfers between devices, local(): lax.all_to_all(partial_value.reshape(devices, tok_rows, features), 'ep',...  5.18 us
  transfers between devices with their start and end apart: 1, of which 1 were waited for; matrix products, arithmetic and copies ran while one was open for 0% of the time, Pallas kernels for 0%

commit v1 on v0

--- a/solution.py
+++ b/solution.py
@@ -36,7 +36,20 @@
     outgoing = jnp.broadcast_to(outbox[:, None], (EXPERTS, partners, tok_rows, features)).reshape(
         devices, tok_rows, features
     )
-    received = lax.all_to_all(outgoing, "ep", split_axis=0, concat_axis=0, tiled=True)
+    x_now, extra = (lax.axis_size("ep"), lax.axis_index("ep"))
+    field_out = list(outgoing.shape)
+    item_now = outgoing.shape[0] // x_now
+    field_out[0] = item_now
+    h_now = field_out[0]
+    field_out[0] = h_now * x_now
+    received = jnp.zeros(field_out, outgoing.dtype)
+    for dd in tuple(range(x_now)):
+        reached = lax.dynamic_slice_in_dim(outgoing, (extra ^ dd) * item_now, item_now, axis=0)
+        if dd:
+            reached = lax.ppermute(
+                reached, axis_name="ep", perm=[(rr, rr ^ dd) for rr in range(x_now)]
+            )
+        received = lax.dynamic_update_slice_in_dim(received, reached, (extra ^ dd) * h_now, axis=0)
     flat_rows = received.reshape(all_rows, features)
     partial_value = expert_rows(flat_rows, w_gate, w_up, w_down)
     returned = lax.all_to_all(

time: 114 us -> 118 us (1.035)
  blocking collectives: 42.4 us -> 0 us
  waiting for transfers between devices: 36 us -> 61 us
  starting transfers between devices: 5.18 us -> 25 us
    all_to_all x1 -> x0, blocking collectives: 42.4 us -> none  [local(): lax.all_to_all(outgoing, 'ep', split_axis=0, concat_axis=0, tiled=True)]
    ppermute x0 -> x15, waiting for transfers between devices: none -> 25 us  [local(): lax.ppermute(reached, axis_name='ep', perm=[(rr, rr ^ dd) for rr in range...]
    ppermute x0 -> x15, starting transfers between devices: none -> 19.1 us  [local(): lax.ppermute(reached, axis_name='ep', perm=[(rr, rr ^ dd) for rr in range...]
  transfers between devices with their start and end apart: 1 -> 16, of which waited for: 1 -> 10; matrix products, arithmetic and copies ran while one was open for 0% -> 0% of each run, Pallas kernels for 0% -> 0%
where the time goes in v1:
time: 118 us; the launch traced here: 117 us
  waiting for transfers between devices  61 us (52%)
  matrix products  25 us (21%)
  starting transfers between devices  25 us (21%)
  local copies, waits for them, and re-layouts  3.32 us (3%)
  other arithmetic  2.14 us (2%)
    all_to_all x1, waiting for transfers between devices, local(): lax.all_to_all(partial_value.reshape(devices, tok_rows, features), 'ep',...  36 us
    ppermute x15, waiting for transfers between devices, local(): lax.ppermute(reached, axis_name='ep', perm=[(rr, rr ^ dd) for rr in range...  25 us
    ppermute x15, starting transfers between devices, local(): lax.ppermute(reached, axis_name='ep', perm=[(rr, rr ^ dd) for rr in range...  19.1 us
    dot_general x1, matrix products, expert_rows(): jnp.dot(hidden, w_down, preferred_element_type=jnp.float32)  16.9 us
    dot_general x1, matrix products, expert_rows(): gate = jnp.dot(row_block, w_gate, preferred_element_type=jnp.float32)  7.77 us
    all_to_all x1, starting transfers between devices, local(): lax.all_to_all(partial_value.reshape(devices, tok_rows, features), 'ep',...  5.93 us
  transfers between devices with their start and end apart: 16, of which 10 were waited for; matrix products, arithmetic and copies ran while one was open for 0% of the time, Pallas kernels for 0%

profile of v1, /device:TPU:15, one launch (start us, length us, event | category | flops | bytes accessed | tf_op | source)
XLA Modules:
  0.0 117.3 jit_solution(16067100868138944885)
XLA Ops:
  0.7 0.1 broadcast_in_dim.46.clone
  0.8 0.1 and.12
  0.9 0.8 copy.24
  1.6 0.1 eq.30
  1.7 0.1 fusion.8
  1.9 0.2 select_reduce_fusion
  2.0 0.1 reshape.33
  2.1 0.1 copy.26
  2.2 0.7 broadcast_maximum_fusion
  2.9 0.1 fusion.6
  3.0 0.3 convolution_convert_fusion.1
  3.3 0.2 broadcast_in_dim.49
  3.5 0.2 broadcast_in_dim.45
  3.7 0.2 constant_dynamic-slice_fusion
  3.9 0.7 collective-permute-start
  4.7 0.3 collective-permute-start.1
  4.9 1.5 %collective-permute-start.2 = (bf16[1,16,3072]{2,1,0:T(8,128)(2,1)S(1)}, bf16[1,16,3072]{2,1,0:T(8,128)(2,1)S(1)}, u32[]{:S(2)}, u32[]{:S(2)}) collective-permute-start(bf16[1,16,3072]{2,1,0:T(8,128)(2,1)S(1)} %get-tuple-element.19), channel_id=1, source_target_pairs={{0,3},{1,2},{2,1},{3,0},{4,7},{5,6},{6,5},{7,4},{8,11},{9,10},{10,... | collective-permute-start | bytes 294920 | tf_op jit(solution)/shard_map/ppermute | solution.py:49
  6.4 0.2 collective-permute-start.3
  6.5 1.6 %collective-permute-start.4 = (bf16[1,16,3072]{2,1,0:T(8,128)(2,1)S(1)}, bf16[1,16,3072]{2,1,0:T(8,128)(2,1)S(1)}, u32[]{:S(2)}, u32[]{:S(2)}) collective-permute-start(bf16[1,16,3072]{2,1,0:T(8,128)(2,1)S(1)} %get-tuple-element.17), channel_id=1, source_target_pairs={{0,5},{1,4},{2,7},{3,6},{4,1},{5,0},{6,3},{7,2},{8,13},{9,12},{10,... | collective-permute-start | bytes 294920 | tf_op jit(solution)/shard_map/ppermute | solution.py:49
  8.2 0.1 collective-permute-start.5
  8.3 0.7 collective-permute-done.1
  9.0 1.8 %collective-permute-start.6 = (bf16[1,16,3072]{2,1,0:T(8,128)(2,1)S(1)}, bf16[1,16,3072]{2,1,0:T(8,128)(2,1)S(1)}, u32[]{:S(2)}, u32[]{:S(2)}) collective-permute-start(bf16[1,16,3072]{2,1,0:T(8,128)(2,1)S(1)} %get-tuple-element.15), channel_id=1, source_target_pairs={{0,7},{1,6},{2,5},{3,4},{4,3},{5,2},{6,1},{7,0},{8,15},{9,14},{10,... | collective-permute-start | bytes 294920 | tf_op jit(solution)/shard_map/ppermute | solution.py:49
  10.9 0.7 collective-permute-done.2
  11.6 2.3 %collective-permute-start.7 = (bf16[1,16,3072]{2,1,0:T(8,128)(2,1)S(1)}, bf16[1,16,3072]{2,1,0:T(8,128)(2,1)S(1)}, u32[]{:S(2)}, u32[]{:S(2)}) collective-permute-start(bf16[1,16,3072]{2,1,0:T(8,128)(2,1)S(1)} %get-tuple-element.14), channel_id=1, source_target_pairs={{0,8},{1,9},{2,10},{3,11},{4,12},{5,13},{6,14},{7,15},{8,0},{9,1},... | collective-permute-start | bytes 294920 | tf_op jit(solution)/shard_map/ppermute | solution.py:49
  13.9 0.4 collective-permute-start.8
  14.4 2.1 %collective-permute-start.9 = (bf16[1,16,3072]{2,1,0:T(8,128)(2,1)S(1)}, bf16[1,16,3072]{2,1,0:T(8,128)(2,1)S(1)}, u32[]{:S(2)}, u32[]{:S(2)}) collective-permute-start(bf16[1,16,3072]{2,1,0:T(8,128)(2,1)S(1)} %get-tuple-element.12), channel_id=1, source_target_pairs={{0,10},{1,11},{2,8},{3,9},{4,14},{5,15},{6,12},{7,13},{8,2},{9,3},... | collective-permute-start | bytes 294920 | tf_op jit(solution)/shard_map/ppermute | solution.py:49
  16.5 5.0 %collective-permute-start.10 = (bf16[1,16,3072]{2,1,0:T(8,128)(2,1)S(1)}, bf16[1,16,3072]{2,1,0:T(8,128)(2,1)S(1)}, u32[]{:S(2)}, u32[]{:S(2)}) collective-permute-start(bf16[1,16,3072]{2,1,0:T(8,128)(2,1)S(1)} %get-tuple-element.11), channel_id=1, source_target_pairs={{0,11},{1,10},{2,9},{3,8},{4,15},{5,14},{6,13},{7,12},{8,3},{9,2},... | collective-permute-start | bytes 294920 | tf_op jit(solution)/shard_map/ppermute | solution.py:49
  21.6 0.6 collective-permute-start.11
  22.2 0.1 collective-permute-start.12
  22.3 7.6 %collective-permute-done.8 = bf16[1,16,3072]{2,1,0:T(8,128)(2,1)S(1)} collective-permute-done((bf16[1,16,3072]{2,1,0:T(8,128)(2,1)S(1)}, bf16[1,16,3072]{2,1,0:T(8,128)(2,1)S(1)}, u32[]{:S(2)}, u32[]{:S(2)}) %collective-permute-start.8) | collective-permute-done | bytes 98336 | tf_op jit(solution)/shard_map/ppermute | solution.py:49
  30.0 2.1 %collective-permute-done.9 = bf16[1,16,3072]{2,1,0:T(8,128)(2,1)S(1)} collective-permute-done((bf16[1,16,3072]{2,1,0:T(8,128)(2,1)S(1)}, bf16[1,16,3072]{2,1,0:T(8,128)(2,1)S(1)}, u32[]{:S(2)}, u32[]{:S(2)}) %collective-permute-start.9) | collective-permute-done | bytes 98336 | tf_op jit(solution)/shard_map/ppermute | solution.py:49
  32.1 2.3 %collective-permute-start.14 = (bf16[1,16,3072]{2,1,0:T(8,128)(2,1)S(1)}, bf16[1,16,3072]{2,1,0:T(8,128)(2,1)S(1)}, u32[]{:S(2)}, u32[]{:S(2)}) collective-permute-start(bf16[1,16,3072]{2,1,0:T(8,128)(2,1)S(1)} %get-tuple-element.7), channel_id=1, source_target_pairs={{0,15},{1,14},{2,13},{3,12},{4,11},{5,10},{6,9},{7,8},{8,7},{9,6},... | collective-permute-start | bytes 294920 | tf_op jit(solution)/shard_map/ppermute | solution.py:49
  34.4 2.8 %collective-permute-done.10 = bf16[1,16,3072]{2,1,0:T(8,128)(2,1)S(1)} collective-permute-done((bf16[1,16,3072]{2,1,0:T(8,128)(2,1)S(1)}, bf16[1,16,3072]{2,1,0:T(8,128)(2,1)S(1)}, u32[]{:S(2)}, u32[]{:S(2)}) %collective-permute-start.10) | collective-permute-done | bytes 98336 | tf_op jit(solution)/shard_map/ppermute | solution.py:49
  37.2 4.4 %collective-permute-done.11 = bf16[1,16,3072]{2,1,0:T(8,128)(2,1)S(1)} collective-permute-done((bf16[1,16,3072]{2,1,0:T(8,128)(2,1)S(1)}, bf16[1,16,3072]{2,1,0:T(8,128)(2,1)S(1)}, u32[]{:S(2)}, u32[]{:S(2)}) %collective-permute-start.11) | collective-permute-done | bytes 98336 | tf_op jit(solution)/shard_map/ppermute | solution.py:49
  41.6 2.6 %collective-permute-done.12 = bf16[1,16,3072]{2,1,0:T(8,128)(2,1)S(1)} collective-permute-done((bf16[1,16,3072]{2,1,0:T(8,128)(2,1)S(1)}, bf16[1,16,3072]{2,1,0:T(8,128)(2,1)S(1)}, u32[]{:S(2)}, u32[]{:S(2)}) %collective-permute-start.12) | collective-permute-done | bytes 98336 | tf_op jit(solution)/shard_map/ppermute | solution.py:49
  44.2 1.6 %collective-permute-done.13 = bf16[1,16,3072]{2,1,0:T(8,128)(2,1)S(1)} collective-permute-done((bf16[1,16,3072]{2,1,0:T(8,128)(2,1)S(1)}, bf16[1,16,3072]{2,1,0:T(8,128)(2,1)S(1)}, u32[]{:S(2)}, u32[]{:S(2)}) %collective-permute-start.13) | collective-permute-done | bytes 98336 | tf_op jit(solution)/shard_map/ppermute | solution.py:49
  45.8 2.5 %collective-permute-done.14 = bf16[1,16,3072]{2,1,0:T(8,128)(2,1)S(1)} collective-permute-done((bf16[1,16,3072]{2,1,0:T(8,128)(2,1)S(1)}, bf16[1,16,3072]{2,1,0:T(8,128)(2,1)S(1)}, u32[]{:S(2)}, u32[]{:S(2)}) %collective-permute-start.14) | collective-permute-done | bytes 98336 | tf_op jit(solution)/shard_map/ppermute | solution.py:49
  48.2 7.8 %fusion.13 = f32[256,2048]{1,0:T(8,128)} fusion(bf16[256,3072]{1,0:T(8,128)(2,1)S(1)} %bitcast.39, bf16[3072,2048]{1,0:T(8,128)(2,1)} %param.11), kind=kOutput, calls=%fused_computation.59 | convolution fusion | flops 3221225472 | bytes 16252928 | tf_op jit(solution)/shard_map/dot_general | solution.py:10
  56.0 16.9 %convolution_convert_fusion = bf16[256,3072]{1,0:T(8,128)(2,1)} fusion(bf16[2048,3072]{1,0:T(8,128)(2,1)} %param.13, f32[256,2048]{1,0:T(8,128)} %fusion.13, bf16[256,3072]{1,0:T(8,128)(2,1)S(1)} %bitcast.40, bf16[3072,2048]{1,0:T(8,128)(2,1)} %param.12), kind=kOutput, calls=%fused_computation.1 | convolution fusion | flops 6446383104 | bytes 30408704 | tf_op jit(solution)/shard_map/dot_general | solution.py:13
  72.9 5.9 %all-to-all-start = ((bf16[16,16,3072]{2,1,0:T(8,128)(2,1)}), bf16[16,16,3072]{2,1,0:T(8,128)(2,1)S(1)}, u32[]{:S(2)}, u32[]{:S(2)}) async-start(bf16[16,16,3072]{2,1,0:T(8,128)(2,1)} %bitcast.5), calls=%async_computation | async-start | bytes 3145728 | tf_op jit(solution)/shard_map/all_to_all | solution.py:55
  78.8 0.1 copy.27
  78.9 0.1 reshape.41
  79.0 36.0 %all-to-all-done = bf16[16,16,3072]{2,1,0:T(8,128)(2,1)S(1)} async-done(((bf16[16,16,3072]{2,1,0:T(8,128)(2,1)}), bf16[16,16,3072]{2,1,0:T(8,128)(2,1)S(1)}, u32[]{:S(2)}, u32[]{:S(2)}) %all-to-all-start) | async-done | bytes 1572896 | tf_op jit(solution)/shard_map/all_to_all | solution.py:55
  115.0 0.2 convert_reduce_fusion
  115.3 0.7 gather_fusion
  116.0 0.2 reshape.40
  116.2 0.3 fusion.10
  116.5 0.8 fusion.4
  (30 shorter events, 0.3 us)
Async XLA Ops:
  0.0 3.0 %copy-start = (bf16[16,3072]{1,0:T(8,128)(2,1)S(1)}, bf16[16,3072]{1,0:T(8,128)(2,1)}, u32[]{:S(2)}) copy-start(bf16[16,3072]{1,0:T(8,128)(2,1)} %param.7) | copy-start | bytes 294916
  3.9 4.2 %collective-permute-start = (bf16[1,16,3072]{2,1,0:T(8,128)(2,1)S(1)}, bf16[1,16,3072]{2,1,0:T(8,128)(2,1)S(1)}, u32[]{:S(2)}, u32[]{:S(2)}) collective-permute-start(bf16[1,16,3072]{2,1,0:T(8,128)(2,1)S(1)} %get-tuple-element.21), channel_id=1, source_target_pairs={{0,1},{1,0},{2,3},{3,2},{4,5},{5,4},{6,7},{7,6},{8,9},{9,8},{10,11... | collective-permute-start | bytes 294920 | tf_op jit(solution)/shard_map/ppermute | solution.py:49
  4.7 4.4 %collective-permute-start.1 = (bf16[1,16,3072]{2,1,0:T(8,128)(2,1)S(1)}, bf16[1,16,3072]{2,1,0:T(8,128)(2,1)S(1)}, u32[]{:S(2)}, u32[]{:S(2)}) collective-permute-start(bf16[1,16,3072]{2,1,0:T(8,128)(2,1)S(1)} %get-tuple-element.20), channel_id=1, source_target_pairs={{0,2},{1,3},{2,0},{3,1},{4,6},{5,7},{6,4},{7,5},{8,10},{9,11},{10,... | collective-permute-start | bytes 294920 | tf_op jit(solution)/shard_map/ppermute | solution.py:49
  4.9 6.7 %collective-permute-start.2 = (bf16[1,16,3072]{2,1,0:T(8,128)(2,1)S(1)}, bf16[1,16,3072]{2,1,0:T(8,128)(2,1)S(1)}, u32[]{:S(2)}, u32[]{:S(2)}) collective-permute-start(bf16[1,16,3072]{2,1,0:T(8,128)(2,1)S(1)} %get-tuple-element.19), channel_id=1, source_target_pairs={{0,3},{1,2},{2,1},{3,0},{4,7},{5,6},{6,5},{7,4},{8,11},{9,10},{10,... | collective-permute-start | bytes 294920 | tf_op jit(solution)/shard_map/ppermute | solution.py:49
  6.4 7.6 %collective-permute-start.3 = (bf16[1,16,3072]{2,1,0:T(8,128)(2,1)S(1)}, bf16[1,16,3072]{2,1,0:T(8,128)(2,1)S(1)}, u32[]{:S(2)}, u32[]{:S(2)}) collective-permute-start(bf16[1,16,3072]{2,1,0:T(8,128)(2,1)S(1)} %get-tuple-element.18), channel_id=1, source_target_pairs={{0,4},{1,5},{2,6},{3,7},{4,0},{5,1},{6,2},{7,3},{8,12},{9,13},{10,... | collective-permute-start | bytes 294920 | tf_op jit(solution)/shard_map/ppermute | solution.py:49
  6.5 7.8 %collective-permute-start.4 = (bf16[1,16,3072]{2,1,0:T(8,128)(2,1)S(1)}, bf16[1,16,3072]{2,1,0:T(8,128)(2,1)S(1)}, u32[]{:S(2)}, u32[]{:S(2)}) collective-permute-start(bf16[1,16,3072]{2,1,0:T(8,128)(2,1)S(1)} %get-tuple-element.17), channel_id=1, source_target_pairs={{0,5},{1,4},{2,7},{3,6},{4,1},{5,0},{6,3},{7,2},{8,13},{9,12},{10,... | collective-permute-start | bytes 294920 | tf_op jit(solution)/shard_map/ppermute | solution.py:49
  8.2 8.4 %collective-permute-start.5 = (bf16[1,16,3072]{2,1,0:T(8,128)(2,1)S(1)}, bf16[1,16,3072]{2,1,0:T(8,128)(2,1)S(1)}, u32[]{:S(2)}, u32[]{:S(2)}) collective-permute-start(bf16[1,16,3072]{2,1,0:T(8,128)(2,1)S(1)} %get-tuple-element.16), channel_id=1, source_target_pairs={{0,6},{1,7},{2,4},{3,5},{4,2},{5,3},{6,0},{7,1},{8,14},{9,15},{10,... | collective-permute-start | bytes 294920 | tf_op jit(solution)/shard_map/ppermute | solution.py:49
  9.0 12.6 %collective-permute-start.6 = (bf16[1,16,3072]{2,1,0:T(8,128)(2,1)S(1)}, bf16[1,16,3072]{2,1,0:T(8,128)(2,1)S(1)}, u32[]{:S(2)}, u32[]{:S(2)}) collective-permute-start(bf16[1,16,3072]{2,1,0:T(8,128)(2,1)S(1)} %get-tuple-element.15), channel_id=1, source_target_pairs={{0,7},{1,6},{2,5},{3,4},{4,3},{5,2},{6,1},{7,0},{8,15},{9,14},{10,... | collective-permute-start | bytes 294920 | tf_op jit(solution)/shard_map/ppermute | solution.py:49
  11.6 10.6 %collective-permute-start.7 = (bf16[1,16,3072]{2,1,0:T(8,128)(2,1)S(1)}, bf16[1,16,3072]{2,1,0:T(8,128)(2,1)S(1)}, u32[]{:S(2)}, u32[]{:S(2)}) collective-permute-start(bf16[1,16,3072]{2,1,0:T(8,128)(2,1)S(1)} %get-tuple-element.14), channel_id=1, source_target_pairs={{0,8},{1,9},{2,10},{3,11},{4,12},{5,13},{6,14},{7,15},{8,0},{9,1},... | collective-permute-start | bytes 294920 | tf_op jit(solution)/shard_map/ppermute | solution.py:49
  13.9 16.0 %collective-permute-start.8 = (bf16[1,16,3072]{2,1,0:T(8,128)(2,1)S(1)}, bf16[1,16,3072]{2,1,0:T(8,128)(2,1)S(1)}, u32[]{:S(2)}, u32[]{:S(2)}) collective-permute-start(bf16[1,16,3072]{2,1,0:T(8,128)(2,1)S(1)} %get-tuple-element.13), channel_id=1, source_target_pairs={{0,9},{1,8},{2,11},{3,10},{4,13},{5,12},{6,15},{7,14},{8,1},{9,0},... | collective-permute-start | bytes 294920 | tf_op jit(solution)/shard_map/ppermute | solution.py:49
  14.4 17.7 %collective-permute-start.9 = (bf16[1,16,3072]{2,1,0:T(8,128)(2,1)S(1)}, bf16[1,16,3072]{2,1,0:T(8,128)(2,1)S(1)}, u32[]{:S(2)}, u32[]{:S(2)}) collective-permute-start(bf16[1,16,3072]{2,1,0:T(8,128)(2,1)S(1)} %get-tuple-element.12), channel_id=1, source_target_pairs={{0,10},{1,11},{2,8},{3,9},{4,14},{5,15},{6,12},{7,13},{8,2},{9,3},... | collective-permute-start | bytes 294920 | tf_op jit(solution)/shard_map/ppermute | solution.py:49
  16.5 20.7 %collective-permute-start.10 = (bf16[1,16,3072]{2,1,0:T(8,128)(2,1)S(1)}, bf16[1,16,3072]{2,1,0:T(8,128)(2,1)S(1)}, u32[]{:S(2)}, u32[]{:S(2)}) collective-permute-start(bf16[1,16,3072]{2,1,0:T(8,128)(2,1)S(1)} %get-tuple-element.11), channel_id=1, source_target_pairs={{0,11},{1,10},{2,9},{3,8},{4,15},{5,14},{6,13},{7,12},{8,3},{9,2},... | collective-permute-start | bytes 294920 | tf_op jit(solution)/shard_map/ppermute | solution.py:49
  21.6 20.0 %collective-permute-start.11 = (bf16[1,16,3072]{2,1,0:T(8,128)(2,1)S(1)}, bf16[1,16,3072]{2,1,0:T(8,128)(2,1)S(1)}, u32[]{:S(2)}, u32[]{:S(2)}) collective-permute-start(bf16[1,16,3072]{2,1,0:T(8,128)(2,1)S(1)} %get-tuple-element.10), channel_id=1, source_target_pairs={{0,12},{1,13},{2,14},{3,15},{4,8},{5,9},{6,10},{7,11},{8,4},{9,5},... | collective-permute-start | bytes 294920 | tf_op jit(solution)/shard_map/ppermute | solution.py:49
  22.2 21.9 %collective-permute-start.12 = (bf16[1,16,3072]{2,1,0:T(8,128)(2,1)S(1)}, bf16[1,16,3072]{2,1,0:T(8,128)(2,1)S(1)}, u32[]{:S(2)}, u32[]{:S(2)}) collective-permute-start(bf16[1,16,3072]{2,1,0:T(8,128)(2,1)S(1)} %get-tuple-element.9), channel_id=1, source_target_pairs={{0,13},{1,12},{2,15},{3,14},{4,9},{5,8},{6,11},{7,10},{8,5},{9,4},... | collective-permute-start | bytes 294920 | tf_op jit(solution)/shard_map/ppermute | solution.py:49
  30.0 15.8 %collective-permute-start.13 = (bf16[1,16,3072]{2,1,0:T(8,128)(2,1)S(1)}, bf16[1,16,3072]{2,1,0:T(8,128)(2,1)S(1)}, u32[]{:S(2)}, u32[]{:S(2)}) collective-permute-start(bf16[1,16,3072]{2,1,0:T(8,128)(2,1)S(1)} %get-tuple-element.8), channel_id=1, source_target_pairs={{0,14},{1,15},{2,12},{3,13},{4,10},{5,11},{6,8},{7,9},{8,6},{9,7},... | collective-permute-start | bytes 294920 | tf_op jit(solution)/shard_map/ppermute | solution.py:49
  32.1 16.2 %collective-permute-start.14 = (bf16[1,16,3072]{2,1,0:T(8,128)(2,1)S(1)}, bf16[1,16,3072]{2,1,0:T(8,128)(2,1)S(1)}, u32[]{:S(2)}, u32[]{:S(2)}) collective-permute-start(bf16[1,16,3072]{2,1,0:T(8,128)(2,1)S(1)} %get-tuple-element.7), channel_id=1, source_target_pairs={{0,15},{1,14},{2,13},{3,12},{4,11},{5,10},{6,9},{7,8},{8,7},{9,6},... | collective-permute-start | bytes 294920 | tf_op jit(solution)/shard_map/ppermute | solution.py:49
  72.9 6.1 %copy-start.1 = (f32[16,2]{0,1:T(2,128)S(1)}, f32[16,2]{0,1:T(2,128)}, u32[]{:S(2)}) copy-start(f32[16,2]{0,1:T(2,128)} %param.9) | copy-start | bytes 388
  72.9 42.1 %all-to-all-start = ((bf16[16,16,3072]{2,1,0:T(8,128)(2,1)}), bf16[16,16,3072]{2,1,0:T(8,128)(2,1)S(1)}, u32[]{:S(2)}, u32[]{:S(2)}) async-start(bf16[16,16,3072]{2,1,0:T(8,128)(2,1)} %bitcast.5), calls=%async_computation | async-start | bytes 3145728 | tf_op jit(solution)/shard_map/all_to_all | solution.py:55
